TPU v7x, 32 devices: a whole 2x2x4 slice. The times are simulated.
32 devices in a mesh: pp: 4 (over y, x), cp: 4 (over z), tp: 2 (over core).
Axes of the slice: x: 2, y: 2, z: 4, core: 2. Of those that a mesh axis runs over, the one named last changes fastest.
Arguments:
- queries: bfloat16 [2048, 16384], P(('pp', 'cp'), 'tp'), may hold values from -12 to 12
- keys: bfloat16 [2048, 1024], P(('pp', 'cp'), 'tp'), may hold values from -12 to 12
- values: bfloat16 [2048, 1024], P(('pp', 'cp'), 'tp'), may hold values from -6 to 6
- pair_order: int32 [4, 4], replicated, may hold values from 0 to 3, each once within a row
- lengths: int32 [4, 2], replicated, may hold values from 128 to 256
- routes: int32 [4, 512, 1], P(None, 'cp'), may hold values from 0 to 7; in each aligned block of 128 rows (0 to 127, 128 to 255, ..., all dimensions but the last counted through in order) at most 32 rows name the same one
Outputs:
- rebalanced: bfloat16 [4096, 16384], P(('pp', 'cp', 'tp'))
Inputs may be any that keep to these rules, and one draw needn't show every extreme that they name: `routes`: at most 32 rows of one device's block name the same destination, and in some block one destination is named by exactly 32 rows.
All inputs are finite; a program needn't handle non-finite values.
Results may differ from a plain program's by a relative error of at most 0.003.
Values may be sent and summed in bfloat16 or wider, within the bound.
No kernel may reach another device: no remote copies, remote signals or barrier semaphores. Data moves between devices by JAX's collectives and lax.ppermute only.
A program may use at most 64 MiB of HBM per device.

v0:
```python
import jax
import jax.numpy as jnp
from jax import lax
from jax.sharding import PartitionSpec as P

HD = 128
masked_score = -1e30


def shifted(block, axis, distance):
    devices = range(lax.axis_size(axis))
    route = [((i - distance) % len(devices), i) for i in devices]
    return lax.ppermute(block, axis, route)


def pair_positions(pair_ids, block_len, cycle_size):
    offsets = jnp.arange(block_len, dtype=jnp.int32)
    first_half = pair_ids[:, None] * block_len + offsets[None, :]
    second_half = (2 * cycle_size - 1 - pair_ids)[:, None] * block_len + offsets[None, :]
    return jnp.concatenate([first_half, second_half], axis=1)


def dispatch_rows(attended, targets, dest_count, capacity):
    row_count = attended.shape[0]
    matches = targets[:, None] == jnp.arange(dest_count, dtype=jnp.int32)[None, :]
    row_ids = jnp.arange(row_count, dtype=jnp.int32)
    earlier = (row_ids[None, :] < row_ids[:, None]).astype(jnp.bfloat16)
    before = jnp.dot(earlier, matches.astype(jnp.bfloat16), preferred_element_type=jnp.float32)
    slot_index = jnp.sum(jnp.where(matches, before, 0.0), axis=1).astype(jnp.int32)
    slot_ids = jnp.arange(capacity, dtype=jnp.int32)
    picked_rows = jnp.logical_and(
        jnp.transpose(matches)[:, None, :], slot_index[None, None, :] == slot_ids[None, :, None]
    )
    selector = picked_rows.astype(jnp.bfloat16).reshape(dest_count * capacity, row_count)
    return jnp.dot(selector, attended, preferred_element_type=jnp.float32).astype(jnp.bfloat16)


def spread_rows(buffer, cycle_size, split_size, capacity, width):
    flat_buffer = buffer.reshape(cycle_size * split_size, capacity, width)
    moved = lax.all_to_all(flat_buffer, ("cp", "tp"), split_axis=0, concat_axis=0, tiled=True)
    moved = jnp.transpose(moved.reshape(cycle_size, split_size, capacity, width), (0, 2, 1, 3))
    return moved.reshape(cycle_size * capacity, split_size * width)


def arrange_rows(attended, routes, source, cycle_size, split_size):
    row_count, width = attended.shape
    dest_count = cycle_size * split_size
    capacity = 2 * row_count // dest_count
    targets = lax.dynamic_index_in_dim(routes, source, 0, keepdims=False)[:, 0]
    buffer = dispatch_rows(attended, targets, dest_count, capacity)
    buffer = buffer.reshape(cycle_size, split_size, capacity, width)
    return spread_rows(buffer, cycle_size, split_size, capacity, width)


def body(queries, keys, values, pair_order, lengths, routes):
    cycle_size = lax.axis_size("cp")
    split_size = lax.axis_size("tp")
    section = lax.axis_index("pp")
    place = lax.axis_index("cp")
    row_count = queries.shape[0]
    block_len = row_count // 4
    width = queries.shape[1]
    group_count = keys.shape[1] // HD
    group_size = width // keys.shape[1]
    score_scale = HD ** (-0.5)
    order_row = lax.dynamic_index_in_dim(pair_order, section, 0, keepdims=False)
    own_pair = lax.dynamic_index_in_dim(order_row, place, 0, keepdims=True)
    query_pos = pair_positions(own_pair, block_len, cycle_size).reshape(2 * block_len)
    limits = lax.dynamic_index_in_dim(lengths, section, 0, keepdims=False)
    query_rows = queries.reshape(2, 2 * block_len, group_count, group_size, HD)
    stat_shape = (2, 2 * block_len, group_count, group_size)
    start_state = (
        jnp.full(stat_shape, masked_score, jnp.float32),
        jnp.zeros(stat_shape, jnp.float32),
        jnp.zeros(stat_shape + (HD,), jnp.float32),
    )
    state = start_state
    key_piece = lax.all_gather(keys, "cp", axis=0, tiled=True)
    value_piece = lax.all_gather(values, "cp", axis=0, tiled=True)
    shard_count = key_piece.shape[0] // row_count
    first_shard = jnp.int32(0) // row_count
    for base in range(0, shard_count, 4):
        block = min(4, shard_count - base)
        key_block = key_piece[base * row_count : (base + block) * row_count].reshape(
            block, 2, 2 * block_len, group_count, HD
        )
        value_block = value_piece[base * row_count : (base + block) * row_count].reshape(
            block, 2, 2 * block_len, group_count, HD
        )
        shard_ids = first_shard + base + jnp.arange(block, dtype=jnp.int32)
        key_pos = pair_positions(order_row[shard_ids], block_len, cycle_size).reshape(
            block * 2 * block_len
        )
        allowed = jnp.logical_and(
            key_pos[None, None, :] <= query_pos[None, :, None],
            key_pos[None, None, :] < limits[:, None, None],
        )
        allowed = allowed[:, :, None, None, :]
        scores = jnp.einsum(
            "sqgrd,nskgd->sqgrnk", query_rows, key_block, preferred_element_type=jnp.float32
        )
        scores = scores.reshape(stat_shape + (block * 2 * block_len,)) * score_scale
        running_max, running_total, running_sum = state
        block_max = jnp.max(jnp.where(allowed, scores, masked_score), axis=4)
        new_max = jnp.maximum(running_max, block_max)
        weights = jnp.where(allowed, jnp.exp(scores - new_max[..., None]), 0.0)
        carry_factor = jnp.exp(running_max - new_max)
        running_total = running_total * carry_factor + jnp.sum(weights, axis=4)
        shaped = weights.astype(jnp.bfloat16).reshape(stat_shape + (block, 2 * block_len))
        running_sum = running_sum * carry_factor[..., None] + jnp.einsum(
            "sqgrnk,nskgd->sqgrd", shaped, value_block, preferred_element_type=jnp.float32
        )
        state = (new_max, running_total, running_sum)
    attended = (state[2] / state[1][..., None]).astype(jnp.bfloat16).reshape(row_count, width)
    arranged = arrange_rows(attended, routes, section, cycle_size, split_size)
    return shifted(arranged, "pp", 1)


def solution(mesh):
    placed = (
        P(("pp", "cp"), "tp"),
        P(("pp", "cp"), "tp"),
        P(("pp", "cp"), "tp"),
        P(),
        P(),
        P(None, "cp", None),
    )
    return jax.shard_map(
        body, mesh=mesh, in_specs=placed, out_specs=P(("pp", "cp", "tp"), None), check_vma=False
    )
```

profile of v0, /device:TPU:0, one launch (start us, length us, event | category | flops | bytes accessed | tf_op | source)
XLA Modules:
  0.0 287.3 jit_solution(959507155664328261)
XLA Ops:
  0.0 0.0 copy-start
  0.0 0.0 copy-start.2
  0.0 0.7 copy-done
  0.7 0.1 fusion.9
  0.9 0.7 fusion.14
  1.6 1.3 dynamic_slice.18
  4.1 0.6 gather_fusion
  4.8 0.9 dynamic-slice_reduce_fusion
  5.7 0.1 add_bitcast_fusion
  5.7 0.1 iota_add_fusion
  5.8 0.1 pad_add_fusion
  5.9 0.1 broadcast_compare_fusion
  6.0 0.1 broadcast_compare_fusion.1
  6.1 2.2 copy.30
  8.3 0.0 copy-done.2
  8.3 17.4 %all_gather.6 = bf16[512,512]{1,0:T(8,128)(2,1)S(1)} all-gather(bf16[128,512]{1,0:T(8,128)(2,1)S(1)} %copy-done.2), channel_id=1, replica_groups=mesh['pp'=4,'cp'=4,'tp'=2] {'cp'}, dimensions={0}, use_global_device_ids=true | all-gather | bytes 655360 | tf_op jit(solution)/shard_map/all_gather | solution.py:78
  25.6 0.1 reshape.234
  25.8 0.1 broadcast_and_fusion
  25.9 5.5 %fusion = (f32[2,64,4,16]{1,3,2,0:T(8,128)S(1)}, f32[2,4,4,64,64,16]{4,3,5,2,1,0:T(8,128)S(1)}) fusion(pred[2,64,4,64]{1,3,2,0:T(8,128)(4,1)S(1)} %broadcast_and_fusion, bf16[2,64,4,16,128,1]{4,3,2,1,0,5:T(8,128)(2,1)S(1)} %bitcast.52, bf16[4,2,64,4,128,1]{4,3,2,1,0,5:T(4,128)(2,1)S(1)} %bitcast.54), kind=kOutput, calls=%fused_computation.3 | convolution fusion | flops 543154176 | bytes 11075584 | tf_op jit(solution)/shard_map/sqgrd,nskgd->sqgrnk/dot_general | solution.py:99
  31.4 6.2 %fusion.3 = (f32[2,64,4,16]{1,3,2,0:T(8,128)S(1)}, bf16[2,64,4,16,4,64]{1,5,3,4,2,0:T(8,128)(2,1)}) fusion(f32[2,4,4,64,64,16]{4,3,5,2,1,0:T(8,128)S(1)} %get-tuple-element.12, f32[2,64,4,16]{1,3,2,0:T(8,128)S(1)} %broadcast_maximum_fusion, pred[2,64,4,64]{1,3,2,0:T(8,128)(4,1)S(1)} %broadcast_and_fusion), kind=kLoop, calls=%fused_computation.6 | loop fusion | flops 10477568 | bytes 12681216 | tf_op jit(solution)/shard_map/reduce_sum | solution.py:108
  37.7 0.1 copy.14
  37.8 0.1 copy.17
  38.0 0.0 copy-start.3
  38.0 17.2 %copy.15 = bf16[2,64,4,16,4,64]{5,3,4,1,2,0:T(8,128)(2,1)} copy(bf16[2,64,4,16,4,64]{1,5,3,4,2,0:T(8,128)(2,1)} %get-tuple-element.6) | data formatting | bytes 8388608 | tf_op jit(solution)/shard_map/convert_element_type | solution.py:109
  55.2 0.0 copy-done.3
  55.2 16.2 %all_gather.7 = bf16[512,512]{1,0:T(8,128)(2,1)S(1)} all-gather(bf16[128,512]{1,0:T(8,128)(2,1)S(1)} %copy-done.3), channel_id=1, replica_groups=mesh['pp'=4,'cp'=4,'tp'=2] {'cp'}, dimensions={0}, use_global_device_ids=true | all-gather | bytes 655360 | tf_op jit(solution)/shard_map/all_gather | solution.py:79
  71.4 0.1 reshape.236
  71.6 5.7 %fusion.6 = bf16[2,64,4,16,128]{4,3,1,2,0:T(8,128)(2,1)S(1)} fusion(bf16[2,64,4,16,4,64]{5,3,4,1,2,0:T(8,128)(2,1)} %copy.15, f32[2,64,4,16]{3,1,2,0:T(8,128)S(1)} %copy.17, f32[2,64,4,16]{3,1,2,0:T(8,128)S(1)} %copy.14, bf16[4,2,64,4,128,1]{4,3,2,1,0,5:T(4,128)(2,1)S(1)} %bitcast.56), kind=kOutput, calls=%fused_computation.11 | convolution fusion | flops 540016640 | bytes 6881280 | tf_op jit(solution)/shard_map/sqgrnk,nskgd->sqgrd/dot_general | solution.py:110
  77.3 1.9 copy.18
  79.2 2.8 reshape.237
  82.1 1.2 convolution_convert_fusion
  83.3 97.9 %all_to_all.5 = bf16[8,32,8192]{2,1,0:T(8,128)(2,1)S(1)} all-to-all(bf16[8,32,8192]{2,1,0:T(8,128)(2,1)S(1)} %bitcast.49), channel_id=1, replica_groups=mesh['pp'=4,'cp'=4,'tp'=2] {'cp','tp'}, dimensions={0} | all-to-all | bytes 8388608 | tf_op jit(solution)/shard_map/all_to_all | solution.py:40
  181.2 6.4 %copy.19 = bf16[4,2,32,8192]{3,1,2,0:T(2,128)(2,1)} copy(bf16[4,2,32,8192]{3,2,1,0:T(8,128)(2,1)S(1)} %bitcast.50) | data formatting | bytes 8388608 | tf_op jit(solution)/shard_map/reshape | solution.py:41
  187.6 4.8 %copy.31 = bf16[16,8,2,8192]{3,1,2,0:T(8,128)(2,1)S(1)} copy(bf16[16,8,2,8192]{3,2,1,0:T(2,128)(2,1)} %bitcast.51) | data formatting | bytes 8388608
  192.4 0.0 copy-start.1
  192.4 1.6 collective-permute-start
  194.0 91.3 %collective-permute-done = bf16[128,16384]{1,0:T(8,128)(2,1)S(1)} collective-permute-done((bf16[128,16384]{1,0:T(8,128)(2,1)S(1)}, bf16[128,16384]{1,0:T(8,128)(2,1)S(1)}, u32[]{:S(2)}, u32[]{:S(2)}) %collective-permute-start) | collective-permute-done | bytes 4194336 | tf_op jit(solution)/shard_map/ppermute | solution.py:13
  285.3 2.0 copy.45
  287.3 0.0 copy-done.1
  (11 shorter events, 0.1 us)
Async XLA Ops:
  0.0 0.7 copy-start
  0.0 8.3 %copy-start.2 = (bf16[128,512]{1,0:T(8,128)(2,1)S(1)}, bf16[128,512]{1,0:T(8,128)(2,1)}, u32[]{:S(2)}) copy-start(bf16[128,512]{1,0:T(8,128)(2,1)} %param.7) | copy-start | bytes 393220
  38.0 17.2 %copy-start.3 = (bf16[128,512]{1,0:T(8,128)(2,1)S(1)}, bf16[128,512]{1,0:T(8,128)(2,1)}, u32[]{:S(2)}) copy-start(bf16[128,512]{1,0:T(8,128)(2,1)} %param.8) | copy-start | bytes 393220
  192.4 94.9 %copy-start.1 = (s32[4,128,1]{1,2,0:T(1,128)S(1)}, s32[4,128,1]{1,2,0:T(1,128)}, u32[]{:S(2)}) copy-start(s32[4,128,1]{1,2,0:T(1,128)} %param.11) | copy-start | bytes 6148
  192.4 92.9 %collective-permute-start = (bf16[128,16384]{1,0:T(8,128)(2,1)S(1)}, bf16[128,16384]{1,0:T(8,128)(2,1)S(1)}, u32[]{:S(2)}, u32[]{:S(2)}) collective-permute-start(bf16[128,16384]{1,0:T(8,128)(2,1)S(1)} %bitcast.53), channel_id=1, source_target_pairs={{24,0},{0,8},{8,16},{16,24},{25,1},{1,9},{9,17},{17,25},{26,2},{2,... | collective-permute-start | bytes 12582920 | tf_op jit(solution)/shard_map/ppermute | solution.py:13
where the time goes:
time: 288 us; the launch traced here: 287 us
  blocking collectives  131 us (45%)
  waiting for transfers between devices  91.3 us (32%)
  local copies, waits for them, and re-layouts  42 us (15%)
  matrix products  12.6 us (4%)
  other arithmetic  6.85 us (2%)
    all_to_all x1, blocking collectives, spread_rows(): lax.all_to_all(flat_buffer, ('cp', 'tp'), split_axis=0, concat_axis=0, ti...  97.9 us
    ppermute x1, waiting for transfers between devices, shifted(): return lax.ppermute(block, axis, route)  91.3 us
    all_gather x1, blocking collectives, body(): key_piece = lax.all_gather(keys, 'cp', axis=0, tiled=True)  17.4 us
    convert_element_type x1, local copies, waits for them, and re-layouts, body(): weights.astype(jnp.bfloat16).reshape(stat_shape + (block, 2 * block_len))  17.2 us
    all_gather x1, blocking collectives, body(): value_piece = lax.all_gather(values, 'cp', axis=0, tiled=True)  16.2 us
    unnamed x11, local copies, waits for them, and re-layouts  9.69 us
    reshape x1, local copies, waits for them, and re-layouts, spread_rows(): moved.reshape(cycle_size, split_size, capacity, width)  6.38 us
    reduce_sum x1, other arithmetic, body(): running_total = running_total * carry_factor + jnp.sum(weights, axis=4)  6.22 us
  transfers between devices with their start and end apart: 1, of which 1 were waited for; matrix products, arithmetic and copies ran while one was open for 0% of the time, Pallas kernels for 0%

commit v1 on v0

--- a/solution.py
+++ b/solution.py
@@ -5,6 +5,22 @@
 
 HD = 128
 masked_score = -1e30
+
+
+def collect(x, axis, dim):
+    ways, here, hop = (lax.axis_size(axis), lax.axis_index(axis), x.shape[dim])
+    shape = [n * ways if d == dim else n for d, n in enumerate(x.shape)]
+    full = lax.dynamic_update_slice_in_dim(jnp.zeros(shape, x.dtype), x, here * hop, axis=dim)
+    going_up = going_down = x
+    for far in range(1, ways // 2 + 1):
+        going_up = lax.ppermute(going_up, axis, [(d, (d + 1) % ways) for d in range(ways)])
+        full = lax.dynamic_update_slice_in_dim(full, going_up, (here - far) % ways * hop, axis=dim)
+        if 2 * far < ways:
+            going_down = lax.ppermute(going_down, axis, [(d, (d - 1) % ways) for d in range(ways)])
+            full = lax.dynamic_update_slice_in_dim(
+                full, going_down, (here + far) % ways * hop, axis=dim
+            )
+    return full
 
 
 def shifted(block, axis, distance):
@@ -75,7 +91,7 @@
         jnp.zeros(stat_shape + (HD,), jnp.float32),
     )
     state = start_state
-    key_piece = lax.all_gather(keys, "cp", axis=0, tiled=True)
+    key_piece = collect(keys, "cp", 0)
     value_piece = lax.all_gather(values, "cp", axis=0, tiled=True)
     shard_count = key_piece.shape[0] // row_count
     first_shard = jnp.int32(0) // row_count

time: 288 us -> 282 us (0.979)
  blocking collectives: 131 us -> 112 us
  waiting for transfers between devices: 91.3 us -> 97.7 us
  starting transfers between devices: 1.55 us -> 7.1 us
    all_gather x1 -> x0, blocking collectives: 17.4 us -> none  [body(): key_piece = lax.all_gather(keys, 'cp', axis=0, tiled=True)]
    ppermute x0 -> x3, waiting for transfers between devices: none -> 6.53 us  [the longest x2 6.53 us: collect(): lax.ppermute(going_up, axis, [(d, (d + 1) % ways) for d in range(ways)])]
    ppermute x0 -> x3, starting transfers between devices: none -> 5.3 us  [the longest x2 3.22 us: collect(): lax.ppermute(going_up, axis, [(d, (d + 1) % ways) for d in range(ways)])]
    unnamed x11 -> x9, local copies, waits for them, and re-layouts: 9.69 us -> 9.01 us
  transfers between devices with their start and end apart: 1 -> 4, of which waited for: 1 -> 2; matrix products, arithmetic and copies ran while one was open for 0% -> 3% of each run, Pallas kernels for 0% -> 0%
where the time goes in v1:
time: 282 us; the launch traced here: 281 us
  blocking collectives  112 us (40%)
  waiting for transfers between devices  97.7 us (35%)
  local copies, waits for them, and re-layouts  43.2 us (15%)
  matrix products  12.6 us (4%)
  starting transfers between devices  7.1 us (3%)
  other arithmetic  6.84 us (2%)
    all_to_all x1, blocking collectives, spread_rows(): lax.all_to_all(flat_buffer, ('cp', 'tp'), split_axis=0, concat_axis=0, ti...  96.5 us
    ppermute x1, waiting for transfers between devices, shifted(): return lax.ppermute(block, axis, route)  91.2 us
    convert_element_type x1, local copies, waits for them, and re-layouts, body(): weights.astype(jnp.bfloat16).reshape(stat_shape + (block, 2 * block_len))  17.2 us
    all_gather x1, blocking collectives, body(): value_piece = lax.all_gather(values, 'cp', axis=0, tiled=True)  15.8 us
    unnamed x9, local copies, waits for them, and re-layouts  9.01 us
    ppermute x2, waiting for transfers between devices, collect(): lax.ppermute(going_up, axis, [(d, (d + 1) % ways) for d in range(ways)])  6.53 us
    reshape x1, local copies, waits for them, and re-layouts, spread_rows(): moved.reshape(cycle_size, split_size, capacity, width)  6.38 us
    reduce_sum x1, other arithmetic, body(): running_total = running_total * carry_factor + jnp.sum(weights, axis=4)  6.2 us
  transfers between devices with their start and end apart: 4, of which 2 were waited for; matrix products, arithmetic and copies ran while one was open for 3% of the time, Pallas kernels for 0%

profile of v1, /device:TPU:0, one launch (start us, length us, event | category | flops | bytes accessed | tf_op | source)
XLA Modules:
  0.0 281.2 jit_solution(9802608389377049211)
XLA Ops:
  0.0 0.0 copy-start
  0.0 3.0 %collective-permute-start = (bf16[128,512]{1,0:T(8,128)(2,1)}, bf16[128,512]{1,0:T(8,128)(2,1)S(1)}, u32[]{:S(2)}, u32[]{:S(2)}) collective-permute-start(bf16[128,512]{1,0:T(8,128)(2,1)} %param.7), channel_id=1, source_target_pairs={{0,2},{2,4},{4,6},{6,0},{1,3},{3,5},{5,7},{7,1},{8,10},{10,12},{12... | collective-permute-start | bytes 393224 | tf_op jit(solution)/shard_map/ppermute | solution.py:16
  3.0 2.1 collective-permute-start.1
  5.1 0.0 copy-done
  5.1 0.1 fusion.9
  5.3 0.7 fusion.15
  6.0 1.3 dynamic_slice.18
  8.6 0.6 gather_fusion
  9.2 0.9 fusion.13
  10.1 0.1 add_bitcast_fusion
  10.2 0.1 iota_add_fusion
  10.2 0.1 pad_add_fusion
  10.3 0.1 broadcast_compare_fusion
  10.4 0.1 broadcast_compare_fusion.1
  10.5 0.1 broadcast_and_fusion
  10.7 15.8 %all_gather.3 = bf16[512,512]{1,0:T(8,128)(2,1)S(1)} all-gather(bf16[128,512]{1,0:T(8,128)(2,1)} %param.8), channel_id=1, replica_groups=mesh['pp'=4,'cp'=4,'tp'=2] {'cp'}, dimensions={0}, use_global_device_ids=true | all-gather | bytes 655360 | tf_op jit(solution)/shard_map/all_gather | solution.py:95
  26.5 0.9 constant_dynamic-update-slice_fusion.3
  27.5 2.2 copy.30
  29.7 0.9 reshape.236
  30.6 0.0 collective-permute-done
  30.6 0.2 collective-permute-start.2
  30.8 0.0 collective-permute-done.1
  30.8 6.5 %collective-permute-done.2 = bf16[128,512]{1,0:T(8,128)(2,1)S(1)} collective-permute-done((bf16[128,512]{1,0:T(8,128)(2,1)S(1)}, bf16[128,512]{1,0:T(8,128)(2,1)S(1)}, u32[]{:S(2)}, u32[]{:S(2)}) %collective-permute-start.2) | collective-permute-done | bytes 131104 | tf_op jit(solution)/shard_map/ppermute | solution.py:16
  37.4 0.1 reshape.234
  37.5 5.5 %fusion = (f32[2,64,4,16]{1,3,2,0:T(8,128)S(1)}, f32[2,4,4,64,64,16]{4,3,5,2,1,0:T(8,128)S(1)}) fusion(pred[2,64,4,64]{1,3,2,0:T(8,128)(4,1)S(1)} %broadcast_and_fusion, bf16[2,64,4,16,128,1]{4,3,2,1,0,5:T(8,128)(2,1)S(1)} %bitcast.52, bf16[4,2,64,4,128,1]{4,3,2,1,0,5:T(4,128)(2,1)S(1)} %bitcast.54), kind=kOutput, calls=%fused_computation.3 | convolution fusion | flops 543154176 | bytes 11075584 | tf_op jit(solution)/shard_map/sqgrd,nskgd->sqgrnk/dot_general | solution.py:115
  43.0 6.2 %fusion.3 = (f32[2,64,4,16]{1,3,2,0:T(8,128)S(1)}, bf16[2,64,4,16,4,64]{1,5,3,4,2,0:T(8,128)(2,1)}) fusion(f32[2,4,4,64,64,16]{4,3,5,2,1,0:T(8,128)S(1)} %get-tuple-element.12, f32[2,64,4,16]{1,3,2,0:T(8,128)S(1)} %broadcast_maximum_fusion, pred[2,64,4,64]{1,3,2,0:T(8,128)(4,1)S(1)} %broadcast_and_fusion), kind=kLoop, calls=%fused_computation.6 | loop fusion | flops 10477568 | bytes 12681216 | tf_op jit(solution)/shard_map/reduce_sum | solution.py:124
  49.3 0.1 copy.14
  49.4 0.1 copy.17
  49.5 0.0 copy-start.2
  49.5 17.2 %copy.15 = bf16[2,64,4,16,4,64]{5,3,4,1,2,0:T(8,128)(2,1)} copy(bf16[2,64,4,16,4,64]{1,5,3,4,2,0:T(8,128)(2,1)} %get-tuple-element.6) | data formatting | bytes 8388608 | tf_op jit(solution)/shard_map/convert_element_type | solution.py:125
  66.8 0.0 copy-done.2
  66.8 5.7 %fusion.6 = bf16[2,64,4,16,128]{4,3,1,2,0:T(8,128)(2,1)S(1)} fusion(bf16[2,64,4,16,4,64]{5,3,4,1,2,0:T(8,128)(2,1)} %copy.15, f32[2,64,4,16]{3,1,2,0:T(8,128)S(1)} %copy.17, f32[2,64,4,16]{3,1,2,0:T(8,128)S(1)} %copy.14, bf16[4,2,64,4,128,1]{4,3,2,1,0,5:T(4,128)(2,1)S(1)} %bitcast.56), kind=kOutput, calls=%fused_computation.11 | convolution fusion | flops 540016640 | bytes 6881280 | tf_op jit(solution)/shard_map/sqgrnk,nskgd->sqgrd/dot_general | solution.py:126
  72.5 1.9 copy.18
  74.4 2.8 %reshape.237 = bf16[128,8192]{1,0:T(8,128)(2,1)S(1)} reshape(bf16[2,64,4,16,128]{4,3,2,1,0:T(8,128)(2,1)} %copy.18) | data formatting | bytes 4194304 | tf_op jit(solution)/shard_map/reshape | solution.py:130
  77.3 1.2 convolution_convert_fusion
  78.5 96.5 %all_to_all.5 = bf16[8,32,8192]{2,1,0:T(8,128)(2,1)S(1)} all-to-all(bf16[8,32,8192]{2,1,0:T(8,128)(2,1)S(1)} %bitcast.49), channel_id=1, replica_groups=mesh['pp'=4,'cp'=4,'tp'=2] {'cp','tp'}, dimensions={0} | all-to-all | bytes 8388608 | tf_op jit(solution)/shard_map/all_to_all | solution.py:56
  175.0 6.4 %copy.19 = bf16[4,2,32,8192]{3,1,2,0:T(2,128)(2,1)} copy(bf16[4,2,32,8192]{3,2,1,0:T(8,128)(2,1)S(1)} %bitcast.50) | data formatting | bytes 8388608 | tf_op jit(solution)/shard_map/reshape | solution.py:57
  181.4 4.8 %copy.31 = bf16[16,8,2,8192]{3,1,2,0:T(8,128)(2,1)S(1)} copy(bf16[16,8,2,8192]{3,2,1,0:T(2,128)(2,1)} %bitcast.51) | data formatting | bytes 8388608
  186.2 0.0 copy-start.1
  186.2 1.8 collective-permute-start.3
  188.0 91.2 %collective-permute-done.3 = bf16[128,16384]{1,0:T(8,128)(2,1)S(1)} collective-permute-done((bf16[128,16384]{1,0:T(8,128)(2,1)S(1)}, bf16[128,16384]{1,0:T(8,128)(2,1)S(1)}, u32[]{:S(2)}, u32[]{:S(2)}) %collective-permute-start.3) | collective-permute-done | bytes 4194336 | tf_op jit(solution)/shard_map/ppermute | solution.py:29
  279.2 2.0 copy.49
  281.2 0.0 copy-done.1
  (15 shorter events, 0.2 us)
Async XLA Ops:
  0.0 5.1 %copy-start = (s32[4,128,1]{1,2,0:T(1,128)S(1)}, s32[4,128,1]{1,2,0:T(1,128)}, u32[]{:S(2)}) copy-start(s32[4,128,1]{1,2,0:T(1,128)} %param.11) | copy-start | bytes 6148
  0.0 30.6 %collective-permute-start = (bf16[128,512]{1,0:T(8,128)(2,1)}, bf16[128,512]{1,0:T(8,128)(2,1)S(1)}, u32[]{:S(2)}, u32[]{:S(2)}) collective-permute-start(bf16[128,512]{1,0:T(8,128)(2,1)} %param.7), channel_id=1, source_target_pairs={{0,2},{2,4},{4,6},{6,0},{1,3},{3,5},{5,7},{7,1},{8,10},{10,12},{12... | collective-permute-start | bytes 393224 | tf_op jit(solution)/shard_map/ppermute | solution.py:16
  3.0 27.8 %collective-permute-start.1 = (bf16[128,512]{1,0:T(8,128)(2,1)}, bf16[128,512]{1,0:T(8,128)(2,1)S(1)}, u32[]{:S(2)}, u32[]{:S(2)}) collective-permute-start(bf16[128,512]{1,0:T(8,128)(2,1)} %param.7), channel_id=1, source_target_pairs={{0,6},{2,0},{4,2},{6,4},{1,7},{3,1},{5,3},{7,5},{8,14},{10,8},{12,... | collective-permute-start | bytes 393224 | tf_op jit(solution)/shard_map/ppermute | solution.py:19
  30.6 6.8 %collective-permute-start.2 = (bf16[128,512]{1,0:T(8,128)(2,1)S(1)}, bf16[128,512]{1,0:T(8,128)(2,1)S(1)}, u32[]{:S(2)}, u32[]{:S(2)}) collective-permute-start(bf16[128,512]{1,0:T(8,128)(2,1)S(1)} %collective-permute-done), channel_id=1, source_target_pairs={{0,2},{2,4},{4,6},{6,0},{1,3},{3,5},{5,7},{7,1},{8,10},{10,12},{12... | collective-permute-start | bytes 393224 | tf_op jit(solution)/shard_map/ppermute | solution.py:16
  49.5 17.2 %copy-start.2 = (bf16[4,2,64,4,128]{4,3,2,1,0:T(4,128)(2,1)S(1)}, bf16[4,2,64,4,128]{4,3,2,1,0:T(4,128)(2,1)}, u32[]{:S(2)}) copy-start(bf16[4,2,64,4,128]{4,3,2,1,0:T(4,128)(2,1)} %reshape.236) | copy-start | bytes 1572868
  186.2 95.0 %copy-start.1 = (s32[4,128,1]{1,2,0:T(1,128)S(1)}, s32[4,128,1]{1,2,0:T(1,128)}, u32[]{:S(2)}) copy-start(s32[4,128,1]{1,2,0:T(1,128)} %param.11) | copy-start | bytes 6148
  186.2 93.0 %collective-permute-start.3 = (bf16[128,16384]{1,0:T(8,128)(2,1)S(1)}, bf16[128,16384]{1,0:T(8,128)(2,1)S(1)}, u32[]{:S(2)}, u32[]{:S(2)}) collective-permute-start(bf16[128,16384]{1,0:T(8,128)(2,1)S(1)} %bitcast.53), channel_id=1, source_target_pairs={{24,0},{0,8},{8,16},{16,24},{25,1},{1,9},{9,17},{17,25},{26,2},{2,... | collective-permute-start | bytes 12582920 | tf_op jit(solution)/shard_map/ppermute | solution.py:29
